TPU v7x, 32 devices: a whole 2x2x4 slice. The times are simulated.
32 devices in a mesh: row: 4 (over y, x), query: 8 (over z, core).
Axes of the slice: x: 2, y: 2, z: 4, core: 2. Of those that a mesh axis runs over, the one named last changes fastest.
Arguments:
- logits: float32 [512, 1024], P('row'), may hold values from -9 to 309
- attributes: int32 [3, 16384], P(None, 'query'), may hold values from 0 to 63
- values: int32 [3, 16384], P(None, 'query'), may hold values from 0 to 15
- targets: float32 [16384], P('query'), may hold values from 0.25 to 1.75
Outputs:
- new_rows: float32 [512, 1024], P('row')
- residual: float32 [16384], P('query')
All inputs are finite; a program needn't handle non-finite values.
Results may differ from a plain program's by a relative error of at most 0.0064.
Values sent between devices are 32-bit elements; how exact they have to be, the bound alone decides.
A program may use at most 64 MiB of HBM per device.

v0:
```python
import jax
import jax.numpy as jnp
from jax import lax
from jax.sharding import PartitionSpec as P

VALS = 16


STEP_RATE = 2.0


def group_softmax(logit_rows):
    row_count = logit_rows.shape[0]
    grouped = logit_rows.reshape(row_count, -1, VALS)
    return jax.nn.softmax(grouped, axis=-1).reshape(row_count, -1)


def relaxed_update(logit_rows, relaxed, accumulated):
    row_count = logit_rows.shape[0]
    scaled = float(VALS * VALS) * accumulated
    grouped_p = relaxed.reshape(row_count, -1, VALS)
    grouped_d = scaled.reshape(row_count, -1, VALS)
    weighted_mean = jnp.sum(grouped_p * grouped_d, axis=-1, keepdims=True)
    tangent = (grouped_p * (grouped_d - weighted_mean)).reshape(row_count, -1)
    return group_softmax(logit_rows - STEP_RATE * tangent)


def make_selectors(columns, col_width):
    col_positions = jnp.arange(col_width, dtype=jnp.int32)[:, None]
    return [
        (col_positions == columns[slot_index][None, :]).astype(jnp.bfloat16)
        for slot_index in range(3)
    ]


def pick_columns(relaxed_b, selectors):
    return [
        jnp.dot(relaxed_b, selector, preferred_element_type=jnp.float32) for selector in selectors
    ]


def weight_sums(picked, misfit, selectors, running):
    weights = [
        (picked[1] * picked[2] * misfit).astype(jnp.bfloat16),
        (picked[0] * picked[2] * misfit).astype(jnp.bfloat16),
        (picked[0] * picked[1] * misfit).astype(jnp.bfloat16),
    ]
    for slot_index in range(3):
        running = running + lax.dot_general(
            weights[slot_index],
            selectors[slot_index],
            (((1,), (1,)), ((), ())),
            preferred_element_type=jnp.float32,
        )
    return running


def local(logits, attributes, values, targets):
    row_count, col_width = logits.shape
    total_rows = row_count * lax.axis_size("row")
    answer_scale = float(VALS**3) / total_rows
    relaxed = group_softmax(logits)
    relaxed_b = relaxed.astype(jnp.bfloat16)
    columns = attributes * VALS + values
    selectors = make_selectors(columns, col_width)
    picked = pick_columns(relaxed_b, selectors)
    partial_answers = jnp.sum(picked[0] * picked[1] * picked[2], axis=0)
    answers = lax.psum(partial_answers, "row") * answer_scale
    residual = answers - targets
    accumulated = weight_sums(
        picked, residual[None, :], selectors, jnp.zeros((row_count, col_width), jnp.float32)
    )
    share = lax.psum_scatter(accumulated, "query", scatter_dimension=1, tiled=True)
    share_width = share.shape[1]
    share_start = lax.axis_index("query") * share_width
    logit_share = lax.dynamic_slice_in_dim(logits, share_start, share_width, 1)
    relaxed_share = lax.dynamic_slice_in_dim(relaxed, share_start, share_width, 1)
    updated_share = relaxed_update(logit_share, relaxed_share, share)
    new_rows = lax.all_gather(updated_share, "query", axis=1, tiled=True)
    return (new_rows, residual)


def solution(mesh):
    placed = (P("row", None), P(None, "query"), P(None, "query"), P("query"))
    return jax.shard_map(
        local, mesh=mesh, in_specs=placed, out_specs=(P("row", None), P("query")), check_vma=False
    )
```

profile of v0, /device:TPU:0, one launch (start us, length us, event | category | flops | bytes accessed | tf_op | source)
XLA Modules:
  0.0 93.2 jit_solution(4023043113153630914)
XLA Ops:
  7.2 0.0 reduce-scatter.2.cloned.1.call-start
  7.2 1.2 %copy.6 = f32[128,1024]{0,1:T(8,128)S(1)} copy(f32[128,1024]{1,0:T(8,128)} %param.4) | data formatting | bytes 1048576 | tf_op args[0]
  8.4 0.1 bitcast_reduce_fusion
  8.5 1.5 %fusion.2 = f32[128,64,16]{0,2,1:T(8,128)S(1)} fusion(f32[128,1024]{0,1:T(8,128)S(1)} %copy.6, f32[128,64]{0,1:T(8,128)S(1)} %bitcast_reduce_fusion), kind=kOutput, calls=%fused_computation.2 | output fusion | flops 139279 | bytes 1081344 | tf_op jit(solution)/shard_map/div | solution.py:15
  10.0 0.2 copy.8
  10.2 0.0 copy-start.3
  10.3 0.2 copy.7
  10.5 0.5 copy-done.3
  11.0 0.0 copy-done.4
  11.1 0.3 copy-done
  11.3 0.2 exponential_divide_fusion
  11.5 1.8 %fusion.8 = f32[128,2048]{1,0:T(8,128)S(1)} fusion(s32[2048]{0:T(1024)S(1)} %bitcast.35, f32[128,1024]{1,0:T(8,128)S(1)} %exponential_divide_fusion), kind=kOutput, calls=%fused_computation.11 | convolution fusion | flops 539099136 | bytes 1581056 | tf_op jit(solution)/shard_map/dot_general | solution.py:38
  13.3 1.8 %fusion.4 = f32[128,2048]{1,0:T(8,128)S(1)} fusion(s32[2048]{0:T(1024)S(1)} %bitcast.37, f32[128,1024]{1,0:T(8,128)S(1)} %exponential_divide_fusion), kind=kOutput, calls=%fused_computation.5 | convolution fusion | flops 539099136 | bytes 1581056 | tf_op jit(solution)/shard_map/dot_general | solution.py:38
  15.1 2.8 %multiply_reduce_fusion = (f32[2048]{0:T(1024)S(1)}, f32[128,2048]{1,0:T(8,128)}, f32[128,2048]{1,0:T(8,128)S(1)}) fusion(f32[128,2048]{1,0:T(8,128)S(1)} %fusion.4, f32[128,2048]{1,0:T(8,128)S(1)} %fusion.8, s32[2048]{0:T(1024)S(1)} %bitcast.33, f32[128,1024]{1,0:T(8,128)S(1)} %exponential_divide_fusion), kind=kOutput, calls=%fused_computation.23 | convolution fusion | flops 539883520 | bytes 4734976 | tf_op jit(solution)/shard_map/dot_general | solution.py:38
  17.9 11.5 %psum.7 = f32[2048]{0:T(1024)S(1)} all-reduce(f32[2048]{0:T(1024)S(1)} %get-tuple-element.2), channel_id=1, replica_groups=mesh['row'=4,'query'=8] {'row'}, use_global_device_ids=true, to_apply=%region_3.0 | all-reduce | flops 2048 | bytes 16384 | tf_op jit(solution)/shard_map/psum | solution.py:68
  29.5 0.0 copy-start.6
  29.5 3.2 %fusion.3 = f32[128,1024]{1,0:T(8,128)S(1)} fusion(s32[2048]{0:T(1024)S(1)} %bitcast.38, f32[128,2048]{1,0:T(8,128)} %copy-done.1, f32[128,2048]{1,0:T(8,128)S(1)} %get-tuple-element.7, f32[2048]{0:T(1024)S(1)} %multiply_subtract_fusion.1), kind=kOutput, calls=%fused_computation.4 | convolution fusion | flops 539754496 | bytes 2637824 | tf_op jit(solution)/shard_map/dot_general | solution.py:49
  32.7 1.9 %fusion.5 = f32[128,1024]{1,0:T(8,128)S(1)} fusion(s32[2048]{0:T(1024)S(1)} %bitcast.34, f32[128,2048]{1,0:T(8,128)S(1)} %copy-done.2, f32[2048]{0:T(1024)S(1)} %multiply_subtract_fusion.1), kind=kOutput, calls=%fused_computation.7 | convolution fusion | flops 539492352 | bytes 1589248 | tf_op jit(solution)/shard_map/dot_general | solution.py:49
  34.6 2.7 %fusion.16 = f32[128,1024]{1,0:T(8,128)} fusion(f32[128,1024]{1,0:T(8,128)S(1)} %fusion.5, f32[128,1024]{1,0:T(8,128)S(1)} %fusion.3, s32[2048]{0:T(1024)S(1)} %bitcast.36, f32[128,2048]{1,0:T(8,128)S(1)} %fusion.4, f32[128,2048]{1,0:T(8,128)S(1)} %get-tuple-element.7, f32[2048]{0:T(1024)S(1)} %multiply_subtract_fusion.1), kind=kOutput, calls=%fused_computation.19 | convolution fusion | flops 540016640 | bytes 3686400 | tf_op jit(solution)/shard_map/dot_general | solution.py:49
  37.3 0.0 reduce-scatter.2.cloned.1.call-update
  37.4 30.5 %reduce-scatter.2.cloned.1.call-done = f32[128,128]{1,0:T(8,128)} async-done(((f32[128,1024]{1,0:T(8,128)}), f32[128,128]{1,0:T(8,128)}) %reduce-scatter.2.cloned.1.call-update) | async-done | bytes 65552 | tf_op jit(solution)/shard_map/reduce_scatter | solution.py:73
  67.9 0.9 multiply_multiply_fusion
  68.7 0.1 copy.9
  68.8 0.2 fusion.1
  69.0 0.1 copy.10
  69.1 0.9 multiply_subtract_fusion
  69.9 0.1 copy.11
  70.1 0.2 fusion
  70.3 0.1 copy.12
  70.4 0.1 copy.13
  70.5 15.0 %all_gather.3 = f32[128,1024]{1,0:T(8,128)S(1)} all-gather(f32[128,128]{1,0:T(8,128)S(1)} %exponential_divide_fusion.1), channel_id=1, replica_groups=mesh['row'=4,'query'=8] {'query'}, dimensions={1}, use_global_device_ids=true | all-gather | bytes 589824 | tf_op jit(solution)/shard_map/all_gather | solution.py:79
  85.5 0.8 copy.15
  (16 shorter events, 0.1 us)
Async XLA Ops:
  7.2 60.7 %reduce-scatter.2.cloned.1.call-start = ((), (), s32[]{:S(2)}) async-start(), calls=%async_computation.1 | async-start | bytes 589824 | tf_op jit(solution)/shard_map/reduce_scatter | solution.py:73
  10.2 0.8 copy-start.3
  10.2 0.8 copy-start.4
  10.3 1.1 %copy-start = (f32[128,1024]{1,0:T(8,128)S(1)}, f32[128,1024]{1,0:T(8,128)}, u32[]{:S(2)}) copy-start(f32[128,1024]{1,0:T(8,128)} %param.4) | copy-start | bytes 1572868
  13.3 1.8 %copy-start.1 = (f32[128,2048]{1,0:T(8,128)}, f32[128,2048]{1,0:T(8,128)S(1)}, u32[]{:S(2)}) copy-start(f32[128,2048]{1,0:T(8,128)S(1)} %fusion.8) | copy-start | bytes 3145732
  15.1 14.3 %copy-start.5 = (f32[2048]{0:T(1024)S(1)}, f32[2048]{0:T(1024)}, u32[]{:S(2)}) copy-start(f32[2048]{0:T(1024)} %param.7) | copy-start | bytes 24580
  29.5 5.1 %copy-start.6 = (f32[2048]{0:T(1024)}, f32[2048]{0:T(1024)S(1)}, u32[]{:S(2)}) copy-start(f32[2048]{0:T(1024)S(1)} %multiply_subtract_fusion.1) | copy-start | bytes 24580
  29.5 3.2 %copy-start.2 = (f32[128,2048]{1,0:T(8,128)S(1)}, f32[128,2048]{1,0:T(8,128)}, u32[]{:S(2)}) copy-start(f32[128,2048]{1,0:T(8,128)} %get-tuple-element.3) | copy-start | bytes 3145732
Sparse Core Ops, SparseCore 0:
  37.5 30.3 reduce-scatter.1
where the time goes:
time: 93.5 us; the launch traced here: 93.2 us
  waiting for transfers between devices  30.5 us (33%)
  blocking collectives  26.5 us (28%)
  between operations  14.3 us (15%)
  matrix products  14.2 us (15%)
  other arithmetic  3.85 us (4%)
  local copies, waits for them, and re-layouts  3.71 us (4%)
    reduce_scatter x1, waiting for transfers between devices, local(): lax.psum_scatter(accumulated, 'query', scatter_dimension=1, tiled=True)  30.5 us
    all_gather x1, blocking collectives, local(): new_rows = lax.all_gather(updated_share, 'query', axis=1, tiled=True)  15 us
    psum x1, blocking collectives, local(): answers = lax.psum(partial_answers, 'row') * answer_scale  11.5 us
    dot_general x3, matrix products, weight_sums(): lax.dot_general(weights[slot_index], selectors[slot_index], (((1,), (1,))...  7.81 us
    dot_general x3, matrix products, pick_columns(): jnp.dot(relaxed_b, selector, preferred_element_type=jnp.float32)  6.42 us
    unnamed x16, local copies, waits for them, and re-layouts  2.82 us
  transfers between devices with their start and end apart: 1, of which 1 were waited for; matrix products, arithmetic and copies ran while one was open for 0% of the time, Pallas kernels for 0%

commit v1 on v0

v1 whole, which is shorter than its diff:
```python
import functools

import jax
import jax.numpy as jnp
from jax import lax
from jax.experimental import pallas as pl
from jax.experimental.pallas import tpu as pltpu
from jax.sharding import PartitionSpec as P

VALS = 16
STEP_RATE = 2.0
CHUNK = 256
BLOCK = 256
LANES = 128
MESH = pl.DeviceIdType.MESH


def group_softmax(tall):
    cols, rows = tall.shape
    grouped = tall.reshape(cols // VALS, VALS, rows)
    shifted = jnp.exp(grouped - jnp.max(grouped, axis=1, keepdims=True))
    return (shifted / jnp.sum(shifted, axis=1, keepdims=True)).reshape(cols, rows)


def kernel(
    n_row, n_query, total_rows,
    log_ref, attr_ref, val_ref, tgt_ref, new_ref, res_ref,
    log_t, rel_t, rel_b, sel, pair, wgt, ans, acc, sib, zin, gat,
    ans_send, ans_recv, sib_send, sib_recv, z_send, z_recv, ag_send, ag_recv, fw_send, fw_recv,
):
    me_r = lax.axis_index("row")
    me_q = lax.axis_index("query")
    me_z, core = me_q // 2, me_q % 2
    other = 1 - core
    n_z = n_query // 2
    rows, cols = log_ref.shape
    queries = attr_ref.shape[1]
    half_q = queries // 2
    half_c = cols // 2
    share = half_c // n_z
    per_block = BLOCK // share
    n_block = half_c // BLOCK
    sibling = (me_r, me_z * 2 + other)

    def remote(src, dst, ssem, rsem, device):
        return pltpu.make_async_remote_copy(
            src_ref=src, dst_ref=dst, send_sem=ssem, recv_sem=rsem,
            device_id=device, device_id_type=MESH,
        )

    barrier = pltpu.get_barrier_semaphore()
    for d in range(1, n_row):
        pl.semaphore_signal(barrier, inc=1, device_id=(lax.rem(me_r + d, n_row), me_q), device_id_type=MESH)
    for d in range(1, n_z):
        pl.semaphore_signal(
            barrier, inc=1, device_id=(me_r, lax.rem(me_z + d, n_z) * 2 + core), device_id_type=MESH
        )
    pl.semaphore_signal(barrier, inc=1, device_id=sibling, device_id_type=MESH)

    for b in range(cols // LANES):
        part = slice(b * LANES, (b + 1) * LANES)
        tall = log_ref[:, part].T
        log_t[part, :] = tall
        relaxed = group_softmax(tall)
        rel_t[part, :] = relaxed
        rel_b[:, part] = relaxed.T.astype(jnp.bfloat16)

    positions = lax.broadcasted_iota(jnp.int32, (cols, CHUNK), 0)
    chunks = half_q // CHUNK

    def ans_copy(h, dst_row, slot, d):
        return remote(ans.at[h, slot], ans.at[h, slot], ans_send.at[h, d], ans_recv.at[h, slot], (dst_row, me_q))

    for h in range(2):

        def forward(c, carry, h=h):
            at = pl.multiple_of(h * half_q + c * CHUNK, CHUNK)
            base = pl.multiple_of(at * 3, CHUNK)
            picked = []
            for k in range(3):
                column = attr_ref[k : k + 1, pl.ds(at, CHUNK)] * VALS + val_ref[k : k + 1, pl.ds(at, CHUNK)]
                one_hot = (positions == column).astype(jnp.float32).astype(jnp.bfloat16)
                sel[:, pl.ds(base + k * CHUNK, CHUNK)] = one_hot
                picked.append(jnp.dot(rel_b[...], one_hot, preferred_element_type=jnp.float32))
            first = picked[0] * picked[1]
            pair[:, pl.ds(base, CHUNK)] = picked[1] * picked[2]
            pair[:, pl.ds(base + CHUNK, CHUNK)] = picked[0] * picked[2]
            pair[:, pl.ds(base + 2 * CHUNK, CHUNK)] = first
            partial = jnp.sum(first * picked[2], axis=0, keepdims=True)
            for i in range(CHUNK // LANES):
                ans[h, me_r, pl.ds(c * (CHUNK // LANES) + i, 1), :] = partial[:, i * LANES : (i + 1) * LANES]
            return carry

        lax.fori_loop(0, chunks, forward, 0)
        if h == 0:
            pl.semaphore_wait(barrier, n_row - 1 + n_z)
        for d in range(1, n_row):
            ans_copy(h, lax.rem(me_r + d, n_row), me_r, d).start()

    answer_scale = float(VALS**3) / total_rows
    half_lines = half_q // LANES

    def rows_at(block):
        return pl.ds(pl.multiple_of(block * BLOCK, BLOCK), BLOCK)

    def sums(block, h):
        span = slice(h * 3 * half_q, (h + 1) * 3 * half_q)
        return lax.dot_general(
            sel[rows_at(block), span], wgt[:, span], (((1,), (1,)), ((), ())),
            preferred_element_type=jnp.float32,
        )

    def piece(side, z):
        return pl.ds(pl.multiple_of(side * half_c + z * share, share), share)

    def sib_copy(side, z):
        return remote(acc.at[piece(side, z)], sib.at[z], sib_send.at[z], sib_recv.at[z], sibling)

    def z_copy(dst_z, slot):
        return remote(
            acc.at[piece(core, dst_z)], zin.at[slot], z_send.at[dst_z], z_recv.at[slot], (me_r, dst_z * 2 + core)
        )

    for h in range(2):
        for d in range(1, n_row):
            ans_copy(h, me_r, lax.rem(me_r + n_row - d, n_row), d).wait_recv()
        total = ans[h, 0]
        for r in range(1, n_row):
            total = total + ans[h, r]
        lines = slice(h * half_lines, (h + 1) * half_lines)
        residual = total * answer_scale - tgt_ref[lines, :]
        res_ref[lines, :] = residual
        for line in range(half_lines):
            chunk, inner = divmod(line * LANES, CHUNK)
            for k in range(3):
                start = h * 3 * half_q + (chunk * 3 + k) * CHUNK + inner
                span = slice(start, start + LANES)
                wgt[:, span] = (pair[:, span] * residual[line : line + 1, :]).astype(jnp.bfloat16)
        if h == 0:
            for block in range(2 * n_block):
                acc[rows_at(block), :] = sums(block, 0)
    for b in range(n_block):
        block = other * n_block + b
        acc[rows_at(block), :] += sums(block, 1)
        for i in range(per_block):
            sib_copy(other, b * per_block + i).start()
    for b in range(n_block):
        inner = lax.rem(me_z // per_block + 1 + b, n_block)
        block = core * n_block + inner
        acc[rows_at(block), :] += sums(block, 1)
        for i in range(per_block):
            z = inner * per_block + i
            sib_copy(core, z).wait_recv()
            summed = acc[piece(core, z), :] + sib[z]

            @pl.when(z != me_z)
            def _():
                acc[piece(core, z), :] = summed
                z_copy(z, me_z).start()

            @pl.when(z == me_z)
            def _():
                zin[me_z] = summed

    mine = piece(core, me_z)
    logit_share, relaxed_share = log_t[mine, :], rel_t[mine, :]
    for d in range(1, n_z):
        z_copy(me_z, lax.rem(me_z + d, n_z)).wait_recv()
    accumulated = zin[0]
    for z in range(1, n_z):
        accumulated = accumulated + zin[z]
    grouped_d = (float(VALS * VALS) * accumulated).reshape(share // VALS, VALS, rows)
    grouped_p = relaxed_share.reshape(share // VALS, VALS, rows)
    weighted_mean = jnp.sum(grouped_p * grouped_d, axis=1, keepdims=True)
    tangent = (grouped_p * (grouped_d - weighted_mean)).reshape(share, rows)
    gat[mine, :] = group_softmax(logit_share - STEP_RATE * tangent)

    def ag_copy(dst_z, z):
        return remote(
            gat.at[piece(core, z)], gat.at[piece(core, z)], ag_send.at[dst_z], ag_recv.at[z], (me_r, dst_z * 2 + core)
        )

    def fw_copy(side, z):
        return remote(gat.at[piece(side, z)], gat.at[piece(side, z)], fw_send.at[z], fw_recv.at[z], sibling)

    for d in range(1, n_z):
        ag_copy(lax.rem(me_z + d, n_z), me_z).start()
    fw_copy(core, me_z).start()
    for d in range(1, n_z):
        z = lax.rem(me_z + d, n_z)
        ag_copy(z, z).wait_recv()
        fw_copy(core, z).start()
    for d in range(n_z):
        fw_copy(other, lax.rem(me_z + d, n_z)).wait_recv()
    for b in range(cols // LANES):
        part = slice(b * LANES, (b + 1) * LANES)
        new_ref[:, part] = gat[part, :].T

    for h in range(2):
        for d in range(1, n_row):
            ans_copy(h, lax.rem(me_r + d, n_row), me_r, d).wait_send()
    for z in range(n_z):
        sib_copy(other, z).wait_send()
    for d in range(1, n_z):
        z = lax.rem(me_z + d, n_z)
        z_copy(z, me_z).wait_send()
        ag_copy(z, me_z).wait_send()
    for z in range(n_z):
        fw_copy(core, z).wait_send()


def local(n_row, n_query, logits, attributes, values, targets):
    rows, cols = logits.shape
    queries = attributes.shape[1]
    n_z = n_query // 2
    share = cols // n_query
    dma = pltpu.SemaphoreType.DMA
    vmem = pl.BlockSpec(memory_space=pltpu.VMEM)
    new_rows, residual = pl.pallas_call(
        functools.partial(kernel, n_row, n_query, rows * n_row),
        out_shape=(
            jax.ShapeDtypeStruct((rows, cols), jnp.float32),
            jax.ShapeDtypeStruct((queries // LANES, LANES), jnp.float32),
        ),
        in_specs=[vmem] * 4,
        out_specs=(vmem, vmem),
        scratch_shapes=[
            pltpu.VMEM((cols, rows), jnp.float32),
            pltpu.VMEM((cols, rows), jnp.float32),
            pltpu.VMEM((rows, cols), jnp.bfloat16),
            pltpu.VMEM((cols, 3 * queries), jnp.bfloat16),
            pltpu.VMEM((rows, 3 * queries), jnp.float32),
            pltpu.VMEM((rows, 3 * queries), jnp.bfloat16),
            pltpu.VMEM((2, n_row, queries // 2 // LANES, LANES), jnp.float32),
            pltpu.VMEM((cols, rows), jnp.float32),
            pltpu.VMEM((n_z, share, rows), jnp.float32),
            pltpu.VMEM((n_z, share, rows), jnp.float32),
            pltpu.VMEM((cols, rows), jnp.float32),
            dma((2, n_row)), dma((2, n_row)),
            dma((n_z,)), dma((n_z,)), dma((n_z,)), dma((n_z,)),
            dma((n_z,)), dma((n_z,)), dma((n_z,)), dma((n_z,)),
        ],
        compiler_params=pltpu.CompilerParams(
            collective_id=0, has_side_effects=True, vmem_limit_bytes=48 * 1024 * 1024
        ),
    )(logits, attributes, values, targets.reshape(queries // LANES, LANES))
    return new_rows, residual.reshape(queries)


def solution(mesh):
    placed = (P("row", None), P(None, "query"), P(None, "query"), P("query"))
    return jax.shard_map(
        functools.partial(local, mesh.shape["row"], mesh.shape["query"]),
        mesh=mesh, in_specs=placed, out_specs=(P("row", None), P("query")), check_vma=False,
    )
```

time: 93.5 us -> 34.1 us (0.36)
  waiting for transfers between devices: 30.5 us -> 0 us
  Pallas kernels: 0 us -> 28.4 us
  blocking collectives: 26.5 us -> 0 us
  matrix products: 14.2 us -> 0 us
  between operations: 14.3 us -> 0.65 us
  other arithmetic: 3.85 us -> 0 us
    reduce_scatter x1 -> x0, waiting for transfers between devices: 30.5 us -> none  [local(): lax.psum_scatter(accumulated, 'query', scatter_dimension=1, tiled=True)]
    pallas_call x0 -> x1, Pallas kernels: none -> 28.4 us  [local(): pl.pallas_call(functools.partial(kernel, n_row, n_query, rows * n_row), o...]
    all_gather x1 -> x0, blocking collectives: 15 us -> none  [local(): new_rows = lax.all_gather(updated_share, 'query', axis=1, tiled=True)]
    dot_general x6 -> x0, matrix products: 14.2 us -> none  [the longest x3 7.81 us: weight_sums(): lax.dot_general(weights[slot_index], selectors[slot_index], (((1,), (1,))...]
    psum x1 -> x0, blocking collectives: 11.5 us -> none  [local(): answers = lax.psum(partial_answers, 'row') * answer_scale]
    div x4 -> x0, other arithmetic: 1.86 us -> none  [group_softmax(): return jax.nn.softmax(grouped, axis=-1).reshape(row_count, -1)]
    unnamed x16 -> x10, local copies, waits for them, and re-layouts: 2.82 us -> 4.64 us
    sub x3 -> x0, other arithmetic: 1.03 us -> none  [the longest x1 0.87 us: relaxed_update(): return group_softmax(logit_rows - STEP_RATE * tangent)]
  transfers between devices with their start and end apart: 1 -> 0, of which waited for: 1 -> 0; matrix products, arithmetic and copies ran while one was open for 0% -> 0% of each run, Pallas kernels for 0% -> 0%
where the time goes in v1:
time: 34.1 us; the launch traced here: 33.7 us
  Pallas kernels  28.4 us (83%)
  local copies, waits for them, and re-layouts  4.64 us (14%)
  between operations  0.65 us (2%)
    pallas_call x1, Pallas kernels, local(): pl.pallas_call(functools.partial(kernel, n_row, n_query, rows * n_row), o...  28.4 us
    unnamed x10, local copies, waits for them, and re-layouts  4.64 us

profile of v1, /device:TPU:0, one launch (start us, length us, event | category | flops | bytes accessed | tf_op | source)
XLA Modules:
  0.0 33.7 jit_solution(1684453894207891287)
XLA Ops:
  0.6 0.0 copy-start
  0.6 1.0 %copy-done = f32[128,1024]{1,0:T(8,128)S(1)} copy-done((f32[128,1024]{1,0:T(8,128)S(1)}, f32[128,1024]{1,0:T(8,128)}, u32[]{:S(2)}) %copy-start) | copy-done | bytes 524312
  1.7 0.0 copy-start.1
  1.7 0.8 %copy-done.1 = s32[3,2048]{1,0:T(4,128)S(1)} copy-done((s32[3,2048]{1,0:T(4,128)S(1)}, s32[3,2048]{1,0:T(4,128)}, u32[]{:S(2)}) %copy-start.1) | copy-done | bytes 24600
  2.4 0.0 copy-start.2
  2.4 0.8 %copy-done.2 = s32[3,2048]{1,0:T(4,128)S(1)} copy-done((s32[3,2048]{1,0:T(4,128)S(1)}, s32[3,2048]{1,0:T(4,128)}, u32[]{:S(2)}) %copy-start.2) | copy-done | bytes 24600
  3.2 0.0 copy-start.3
  3.2 0.7 %copy-done.3 = f32[2048]{0:T(1024)S(1)} copy-done((f32[2048]{0:T(1024)S(1)}, f32[2048]{0:T(1024)}, u32[]{:S(2)}) %copy-start.3) | copy-done | bytes 8216
  3.9 28.4 %shard_map.59 = (f32[128,1024]{1,0:T(8,128)S(1)}, f32[16,128]{1,0:T(8,128)S(1)}) custom-call(f32[128,1024]{1,0:T(8,128)S(1)} %copy-done, s32[3,2048]{1,0:T(4,128)S(1)} %copy-done.1, s32[3,2048]{1,0:T(4,128)S(1)} %copy-done.2, f32[16,128]{1,0:T(8,128)S(1)} %bitcast.2), custom_call_target="tpu_custom_call" | custom-call | tf_op jit(solution)/shard_map/pallas_call | solution.py:219
  32.3 0.8 %copy.8 = f32[128,1024]{1,0:T(8,128)} copy(f32[128,1024]{1,0:T(8,128)S(1)} %get-tuple-element.8) | data formatting | bytes 1048576
  33.1 0.6 %copy.9 = f32[2048]{0:T(1024)} copy(f32[2048]{0:T(1024)S(1)} %bitcast.3) | data formatting | bytes 16384
Async XLA Ops:
  0.6 1.0 %copy-start = (f32[128,1024]{1,0:T(8,128)S(1)}, f32[128,1024]{1,0:T(8,128)}, u32[]{:S(2)}) copy-start(f32[128,1024]{1,0:T(8,128)} %log_ref.1) | copy-start | bytes 1572868
  1.7 0.8 %copy-start.1 = (s32[3,2048]{1,0:T(4,128)S(1)}, s32[3,2048]{1,0:T(4,128)}, u32[]{:S(2)}) copy-start(s32[3,2048]{1,0:T(4,128)} %attr_ref.1) | copy-start | bytes 73732
  2.4 0.8 %copy-start.2 = (s32[3,2048]{1,0:T(4,128)S(1)}, s32[3,2048]{1,0:T(4,128)}, u32[]{:S(2)}) copy-start(s32[3,2048]{1,0:T(4,128)} %val_ref.1) | copy-start | bytes 73732
  3.2 0.7 %copy-start.3 = (f32[2048]{0:T(1024)S(1)}, f32[2048]{0:T(1024)}, u32[]{:S(2)}) copy-start(f32[2048]{0:T(1024)} %param.7) | copy-start | bytes 24580

commit v2 on v1

--- a/solution.py
+++ b/solution.py
@@ -24,8 +24,8 @@
 
 def kernel(
     n_row, n_query, total_rows,
-    log_ref, attr_ref, val_ref, tgt_ref, new_ref, res_ref,
-    log_t, rel_t, rel_b, sel, pair, wgt, ans, acc, sib, zin, gat,
+    log_ref, meta_ref, gat, res_ref,
+    tgt_ref, log_t, rel_t, rel_b, sel, pair, wgt, ans, acc, sib, zin,
     ans_send, ans_recv, sib_send, sib_recv, z_send, z_recv, ag_send, ag_recv, fw_send, fw_recv,
 ):
     me_r = lax.axis_index("row")
@@ -34,7 +34,7 @@
     other = 1 - core
     n_z = n_query // 2
     rows, cols = log_ref.shape
-    queries = attr_ref.shape[1]
+    queries = meta_ref.shape[1]
     half_q = queries // 2
     half_c = cols // 2
     share = half_c // n_z
@@ -65,7 +65,9 @@
         rel_t[part, :] = relaxed
         rel_b[:, part] = relaxed.T.astype(jnp.bfloat16)
 
-    positions = lax.broadcasted_iota(jnp.int32, (cols, CHUNK), 0)
+    for line in range(queries // LANES):
+        tgt_ref[line : line + 1, :] = meta_ref[3:4, line * LANES : (line + 1) * LANES]
+    positions = lax.broadcasted_iota(jnp.int32, (cols, CHUNK), 0).astype(jnp.float32)
     chunks = half_q // CHUNK
 
     def ans_copy(h, dst_row, slot, d):
@@ -78,7 +80,7 @@
             base = pl.multiple_of(at * 3, CHUNK)
             picked = []
             for k in range(3):
-                column = attr_ref[k : k + 1, pl.ds(at, CHUNK)] * VALS + val_ref[k : k + 1, pl.ds(at, CHUNK)]
+                column = meta_ref[k : k + 1, pl.ds(at, CHUNK)]
                 one_hot = (positions == column).astype(jnp.float32).astype(jnp.bfloat16)
                 sel[:, pl.ds(base + k * CHUNK, CHUNK)] = one_hot
                 picked.append(jnp.dot(rel_b[...], one_hot, preferred_element_type=jnp.float32))
@@ -192,10 +194,6 @@
         fw_copy(core, z).start()
     for d in range(n_z):
         fw_copy(other, lax.rem(me_z + d, n_z)).wait_recv()
-    for b in range(cols // LANES):
-        part = slice(b * LANES, (b + 1) * LANES)
-        new_ref[:, part] = gat[part, :].T
-
     for h in range(2):
         for d in range(1, n_row):
             ans_copy(h, lax.rem(me_r + d, n_row), me_r, d).wait_send()
@@ -207,6 +205,13 @@
         ag_copy(z, me_z).wait_send()
     for z in range(n_z):
         fw_copy(core, z).wait_send()
+
+
+def finish(tall_ref, misfit_ref, new_ref, res_ref):
+    for b in range(tall_ref.shape[0] // LANES):
+        part = slice(b * LANES, (b + 1) * LANES)
+        new_ref[:, part] = tall_ref[part, :].T
+    res_ref[...] = misfit_ref[...]
 
 
 def local(n_row, n_query, logits, attributes, values, targets):
@@ -216,15 +221,18 @@
     share = cols // n_query
     dma = pltpu.SemaphoreType.DMA
     vmem = pl.BlockSpec(memory_space=pltpu.VMEM)
-    new_rows, residual = pl.pallas_call(
+    columns = (attributes * VALS + values).astype(jnp.float32)
+    meta = jnp.concatenate([columns, targets[None, :]], axis=0)
+    tall, misfit = pl.pallas_call(
         functools.partial(kernel, n_row, n_query, rows * n_row),
         out_shape=(
-            jax.ShapeDtypeStruct((rows, cols), jnp.float32),
+            jax.ShapeDtypeStruct((cols, rows), jnp.float32),
             jax.ShapeDtypeStruct((queries // LANES, LANES), jnp.float32),
         ),
-        in_specs=[vmem] * 4,
+        in_specs=[vmem] * 2,
         out_specs=(vmem, vmem),
         scratch_shapes=[
+            pltpu.VMEM((queries // LANES, LANES), jnp.float32),
             pltpu.VMEM((cols, rows), jnp.float32),
             pltpu.VMEM((cols, rows), jnp.float32),
             pltpu.VMEM((rows, cols), jnp.bfloat16),
@@ -235,7 +243,6 @@
             pltpu.VMEM((cols, rows), jnp.float32),
             pltpu.VMEM((n_z, share, rows), jnp.float32),
             pltpu.VMEM((n_z, share, rows), jnp.float32),
-            pltpu.VMEM((cols, rows), jnp.float32),
             dma((2, n_row)), dma((2, n_row)),
             dma((n_z,)), dma((n_z,)), dma((n_z,)), dma((n_z,)),
             dma((n_z,)), dma((n_z,)), dma((n_z,)), dma((n_z,)),
@@ -243,7 +250,17 @@
         compiler_params=pltpu.CompilerParams(
             collective_id=0, has_side_effects=True, vmem_limit_bytes=48 * 1024 * 1024
         ),
-    )(logits, attributes, values, targets.reshape(queries // LANES, LANES))
+    )(logits, meta)
+    new_rows, residual = pl.pallas_call(
+        finish,
+        out_shape=(
+            jax.ShapeDtypeStruct((rows, cols), jnp.float32),
+            jax.ShapeDtypeStruct((queries // LANES, LANES), jnp.float32),
+        ),
+        in_specs=[vmem, vmem],
+        out_specs=(vmem, vmem),
+        compiler_params=pltpu.CompilerParams(vmem_limit_bytes=4 * 1024 * 1024),
+    )(tall, misfit)
     return new_rows, residual.reshape(queries)
 
 

time: 34.1 us -> 31.5 us (0.924)
  local copies, waits for them, and re-layouts: 4.64 us -> 1.04 us
  other arithmetic: 0 us -> 0.81 us
  Pallas kernels: 28.4 us -> 28.8 us
    unnamed x10 -> x4, local copies, waits for them, and re-layouts: 4.64 us -> 1.04 us
    pallas_call x0 -> x1, Pallas kernels: none -> 1 us  [local(): pl.pallas_call(finish, out_shape=(jax.ShapeDtypeStruct((rows, cols), jnp....]
    convert_element_type x0 -> x1, other arithmetic: none -> 0.79 us  [local(): columns = (attributes * VALS + values).astype(jnp.float32)]
    pallas_call x1, Pallas kernels: 28.4 us -> 27.8 us  [local(): pl.pallas_call(functools.partial(kernel, n_row, n_query, rows * n_row), o...]
where the time goes in v2:
time: 31.5 us; the launch traced here: 31.3 us
  Pallas kernels  28.8 us (91%)
  local copies, waits for them, and re-layouts  1.04 us (3%)
  other arithmetic  0.81 us (3%)
  between operations  0.67 us (2%)
    pallas_call x1, Pallas kernels, local(): pl.pallas_call(functools.partial(kernel, n_row, n_query, rows * n_row), o...  27.8 us
    unnamed x4, local copies, waits for them, and re-layouts  1.04 us
    pallas_call x1, Pallas kernels, local(): pl.pallas_call(finish, out_shape=(jax.ShapeDtypeStruct((rows, cols), jnp....  1 us
    convert_element_type x1, other arithmetic, local(): columns = (attributes * VALS + values).astype(jnp.float32)  0.79 us

profile of v2, /device:TPU:0, one launch (start us, length us, event | category | flops | bytes accessed | tf_op | source)
XLA Modules:
  0.0 31.3 jit_solution(4843323086628427398)
XLA Ops:
  0.6 0.0 copy-start.1
  0.6 0.8 %add_convert_fusion = f32[3,2048]{1,0:T(4,128)S(1)} fusion(s32[3,2048]{1,0:T(4,128)} %param.6, s32[3,2048]{1,0:T(4,128)} %param.5), kind=kLoop, calls=%fused_computation.1 | loop fusion | flops 18432 | bytes 73728 | tf_op jit(solution)/shard_map/convert_element_type | solution.py:224
  1.4 0.0 copy-done.1
  1.5 0.0 copy-start
  1.5 1.0 %copy-done = f32[128,1024]{1,0:T(8,128)S(1)} copy-done((f32[128,1024]{1,0:T(8,128)S(1)}, f32[128,1024]{1,0:T(8,128)}, u32[]{:S(2)}) %copy-start) | copy-done | bytes 524312
  2.5 27.8 %shard_map.59 = (f32[1024,128]{1,0:T(8,128)S(1)}, f32[16,128]{1,0:T(8,128)S(1)}) custom-call(f32[128,1024]{1,0:T(8,128)S(1)} %copy-done, f32[4,2048]{1,0:T(4,128)S(1)} %pad_maximum_fusion.meta_ref), custom_call_target="tpu_custom_call" | custom-call | tf_op jit(solution)/shard_map/pallas_call | solution.py:226
  30.3 1.0 %shard_map.60 = (f32[128,1024]{1,0:T(8,128)}, f32[16,128]{1,0:T(8,128)}) custom-call(f32[1024,128]{1,0:T(8,128)S(1)} %get-tuple-element.6.tall_ref, f32[16,128]{1,0:T(8,128)S(1)} %get-tuple-element.7.misfit_ref), custom_call_target="tpu_custom_call" | custom-call | tf_op jit(solution)/shard_map/pallas_call | solution.py:254
  (1 shorter events, 0.0 us)
Async XLA Ops:
  0.6 0.8 %copy-start.1 = (f32[2048]{0:T(1024)S(1)}, f32[2048]{0:T(1024)}, u32[]{:S(2)}) copy-start(f32[2048]{0:T(1024)} %param.7) | copy-start | bytes 24580
  1.5 1.0 %copy-start = (f32[128,1024]{1,0:T(8,128)S(1)}, f32[128,1024]{1,0:T(8,128)}, u32[]{:S(2)}) copy-start(f32[128,1024]{1,0:T(8,128)} %log_ref.1) | copy-start | bytes 1572868

commit v3 on v2

--- a/solution.py
+++ b/solution.py
@@ -123,6 +123,14 @@
             acc.at[piece(core, dst_z)], zin.at[slot], z_send.at[dst_z], z_recv.at[slot], (me_r, dst_z * 2 + core)
         )
 
+    lower = me_z < n_z // 2
+
+    def inner_at(b):
+        return jnp.where(lower, n_block - 1 - b, b)
+
+    def piece_at(b, i):
+        return inner_at(b) * per_block + jnp.where(lower, per_block - 1 - i, i)
+
     for h in range(2):
         for d in range(1, n_row):
             ans_copy(h, me_r, lax.rem(me_r + n_row - d, n_row), d).wait_recv()
@@ -142,16 +150,15 @@
             for block in range(2 * n_block):
                 acc[rows_at(block), :] = sums(block, 0)
     for b in range(n_block):
-        block = other * n_block + b
+        block = other * n_block + inner_at(b)
         acc[rows_at(block), :] += sums(block, 1)
         for i in range(per_block):
-            sib_copy(other, b * per_block + i).start()
+            sib_copy(other, piece_at(b, i)).start()
     for b in range(n_block):
-        inner = lax.rem(me_z // per_block + 1 + b, n_block)
-        block = core * n_block + inner
+        block = core * n_block + inner_at(b)
         acc[rows_at(block), :] += sums(block, 1)
         for i in range(per_block):
-            z = inner * per_block + i
+            z = piece_at(b, i)
             sib_copy(core, z).wait_recv()
             summed = acc[piece(core, z), :] + sib[z]
 
@@ -177,6 +184,10 @@
     tangent = (grouped_p * (grouped_d - weighted_mean)).reshape(share, rows)
     gat[mine, :] = group_softmax(logit_share - STEP_RATE * tangent)
 
+    def toward(d):
+        sign = jnp.where(me_z < n_z // 2, 1, n_z - 1)
+        return lax.rem(me_z + sign * d, n_z)
+
     def ag_copy(dst_z, z):
         return remote(
             gat.at[piece(core, z)], gat.at[piece(core, z)], ag_send.at[dst_z], ag_recv.at[z], (me_r, dst_z * 2 + core)
@@ -185,15 +196,15 @@
     def fw_copy(side, z):
         return remote(gat.at[piece(side, z)], gat.at[piece(side, z)], fw_send.at[z], fw_recv.at[z], sibling)
 
-    for d in range(1, n_z):
-        ag_copy(lax.rem(me_z + d, n_z), me_z).start()
+    for d in range(n_z - 1, 0, -1):
+        ag_copy(toward(d), me_z).start()
     fw_copy(core, me_z).start()
     for d in range(1, n_z):
-        z = lax.rem(me_z + d, n_z)
+        z = toward(d)
         ag_copy(z, z).wait_recv()
         fw_copy(core, z).start()
     for d in range(n_z):
-        fw_copy(other, lax.rem(me_z + d, n_z)).wait_recv()
+        fw_copy(other, toward(d)).wait_recv()
     for h in range(2):
         for d in range(1, n_row):
             ans_copy(h, lax.rem(me_r + d, n_row), me_r, d).wait_send()

time: 31.5 us -> 31.4 us (level)
  no operation moved by 1% of the time
where the time goes in v3:
time: 31.4 us; the launch traced here: 31.2 us
  Pallas kernels  28.7 us (91%)
  local copies, waits for them, and re-layouts  1.04 us (3%)
  other arithmetic  0.81 us (3%)
  between operations  0.67 us (2%)
    pallas_call x1, Pallas kernels, local(): pl.pallas_call(functools.partial(kernel, n_row, n_query, rows * n_row), o...  27.7 us
    unnamed x4, local copies, waits for them, and re-layouts  1.04 us
    pallas_call x1, Pallas kernels, local(): pl.pallas_call(finish, out_shape=(jax.ShapeDtypeStruct((rows, cols), jnp....  1 us
    convert_element_type x1, other arithmetic, local(): columns = (attributes * VALS + values).astype(jnp.float32)  0.79 us

profile of v3, /device:TPU:0, one launch (start us, length us, event | category | flops | bytes accessed | tf_op | source)
XLA Modules:
  0.0 31.2 jit_solution(11277285644449023380)
XLA Ops:
  0.6 0.0 copy-start.1
  0.6 0.8 %add_convert_fusion = f32[3,2048]{1,0:T(4,128)S(1)} fusion(s32[3,2048]{1,0:T(4,128)} %param.6, s32[3,2048]{1,0:T(4,128)} %param.5), kind=kLoop, calls=%fused_computation.1 | loop fusion | flops 18432 | bytes 73728 | tf_op jit(solution)/shard_map/convert_element_type | solution.py:235
  1.4 0.0 copy-done.1
  1.5 0.0 copy-start
  1.5 1.0 %copy-done = f32[128,1024]{1,0:T(8,128)S(1)} copy-done((f32[128,1024]{1,0:T(8,128)S(1)}, f32[128,1024]{1,0:T(8,128)}, u32[]{:S(2)}) %copy-start) | copy-done | bytes 524312
  2.5 27.7 %shard_map.59 = (f32[1024,128]{1,0:T(8,128)S(1)}, f32[16,128]{1,0:T(8,128)S(1)}) custom-call(f32[128,1024]{1,0:T(8,128)S(1)} %copy-done, f32[4,2048]{1,0:T(4,128)S(1)} %pad_maximum_fusion.meta_ref), custom_call_target="tpu_custom_call" | custom-call | tf_op jit(solution)/shard_map/pallas_call | solution.py:237
  30.2 1.0 %shard_map.60 = (f32[128,1024]{1,0:T(8,128)}, f32[16,128]{1,0:T(8,128)}) custom-call(f32[1024,128]{1,0:T(8,128)S(1)} %get-tuple-element.6.tall_ref, f32[16,128]{1,0:T(8,128)S(1)} %get-tuple-element.7.misfit_ref), custom_call_target="tpu_custom_call" | custom-call | tf_op jit(solution)/shard_map/pallas_call | solution.py:265
  (1 shorter events, 0.0 us)
Async XLA Ops:
  0.6 0.8 %copy-start.1 = (f32[2048]{0:T(1024)S(1)}, f32[2048]{0:T(1024)}, u32[]{:S(2)}) copy-start(f32[2048]{0:T(1024)} %param.7) | copy-start | bytes 24580
  1.5 1.0 %copy-start = (f32[128,1024]{1,0:T(8,128)S(1)}, f32[128,1024]{1,0:T(8,128)}, u32[]{:S(2)}) copy-start(f32[128,1024]{1,0:T(8,128)} %log_ref.1) | copy-start | bytes 1572868

commit v4 on v3

--- a/solution.py
+++ b/solution.py
@@ -147,8 +147,10 @@
                 span = slice(start, start + LANES)
                 wgt[:, span] = (pair[:, span] * residual[line : line + 1, :]).astype(jnp.bfloat16)
         if h == 0:
-            for block in range(2 * n_block):
-                acc[rows_at(block), :] = sums(block, 0)
+            span = slice(0, 3 * half_q)
+            acc[...] = lax.dot_general(
+                sel[:, span], wgt[:, span], (((1,), (1,)), ((), ())), preferred_element_type=jnp.float32
+            )
     for b in range(n_block):
         block = other * n_block + inner_at(b)
         acc[rows_at(block), :] += sums(block, 1)

time: 31.4 us -> 33.5 us (1.067)
  Pallas kernels: 28.7 us -> 30.8 us
    pallas_call x1, Pallas kernels: 27.7 us -> 29.8 us  [local(): pl.pallas_call(functools.partial(kernel, n_row, n_query, rows * n_row), o...]
where the time goes in v4:
time: 33.5 us; the launch traced here: 33.3 us
  Pallas kernels  30.8 us (92%)
  local copies, waits for them, and re-layouts  1.04 us (3%)
  other arithmetic  0.81 us (2%)
  between operations  0.67 us (2%)
    pallas_call x1, Pallas kernels, local(): pl.pallas_call(functools.partial(kernel, n_row, n_query, rows * n_row), o...  29.8 us
    unnamed x4, local copies, waits for them, and re-layouts  1.04 us
    pallas_call x1, Pallas kernels, local(): pl.pallas_call(finish, out_shape=(jax.ShapeDtypeStruct((rows, cols), jnp....  1 us
    convert_element_type x1, other arithmetic, local(): columns = (attributes * VALS + values).astype(jnp.float32)  0.79 us

profile of v4, /device:TPU:0, one launch (start us, length us, event | category | flops | bytes accessed | tf_op | source)
XLA Modules:
  0.0 33.3 jit_solution(1383986445159469269)
XLA Ops:
  0.6 0.0 copy-start.1
  0.6 0.8 %add_convert_fusion = f32[3,2048]{1,0:T(4,128)S(1)} fusion(s32[3,2048]{1,0:T(4,128)} %param.6, s32[3,2048]{1,0:T(4,128)} %param.5), kind=kLoop, calls=%fused_computation.1 | loop fusion | flops 18432 | bytes 73728 | tf_op jit(solution)/shard_map/convert_element_type | solution.py:237
  1.4 0.0 copy-done.1
  1.5 0.0 copy-start
  1.5 1.0 %copy-done = f32[128,1024]{1,0:T(8,128)S(1)} copy-done((f32[128,1024]{1,0:T(8,128)S(1)}, f32[128,1024]{1,0:T(8,128)}, u32[]{:S(2)}) %copy-start) | copy-done | bytes 524312
  2.5 29.8 %shard_map.59 = (f32[1024,128]{1,0:T(8,128)S(1)}, f32[16,128]{1,0:T(8,128)S(1)}) custom-call(f32[128,1024]{1,0:T(8,128)S(1)} %copy-done, f32[4,2048]{1,0:T(4,128)S(1)} %pad_maximum_fusion.meta_ref), custom_call_target="tpu_custom_call" | custom-call | tf_op jit(solution)/shard_map/pallas_call | solution.py:239
  32.3 1.0 %shard_map.60 = (f32[128,1024]{1,0:T(8,128)}, f32[16,128]{1,0:T(8,128)}) custom-call(f32[1024,128]{1,0:T(8,128)S(1)} %get-tuple-element.6.tall_ref, f32[16,128]{1,0:T(8,128)S(1)} %get-tuple-element.7.misfit_ref), custom_call_target="tpu_custom_call" | custom-call | tf_op jit(solution)/shard_map/pallas_call | solution.py:267
  (1 shorter events, 0.0 us)
Async XLA Ops:
  0.6 0.8 %copy-start.1 = (f32[2048]{0:T(1024)S(1)}, f32[2048]{0:T(1024)}, u32[]{:S(2)}) copy-start(f32[2048]{0:T(1024)} %param.7) | copy-start | bytes 24580
  1.5 1.0 %copy-start = (f32[128,1024]{1,0:T(8,128)S(1)}, f32[128,1024]{1,0:T(8,128)}, u32[]{:S(2)}) copy-start(f32[128,1024]{1,0:T(8,128)} %log_ref.1) | copy-start | bytes 1572868
